TPU v7x, 32 devices: a whole 2x2x4 slice. The times are simulated.
32 devices in a mesh: groups: 2 (over y), out: 4 (over z), inp: 4 (over x, core).
Axes of the slice: x: 2, y: 2, z: 4, core: 2. Of those that a mesh axis runs over, the one named last changes fastest.
Arguments:
- acts_rot: bfloat16 [64, 8192], P(('groups', 'out', 'inp')), parts along dimension 0, may hold values from -6 to 6
- grads_rot: bfloat16 [64, 28672], P(('groups', 'out', 'inp')), parts along dimension 0, may hold values from -0.00024414062 to 0.00024414062
- query_grads: bfloat16 [8, 128, 28672], P('groups', None, 'out'), parts along dimension 0, may hold values from -6 to 6
- query_acts: bfloat16 [8, 128, 8192], P('groups', 'out', 'inp'), parts along dimension 0, may hold values from -0.5 to 0.5
- eigen: bfloat16 [28672, 8192], P('out', 'inp'), may hold values from 0.049804688 to 5
- block_mask: int32 [8, 224, 64], P('groups'), parts along dimension 0, may hold values from 0 to 1, as said below
- order: int32 [64], P('groups'), parts along dimension 0, may hold values from 0 to 31, each once
- segment_ids: int32 [64], P('groups'), parts along dimension 0, may hold values from 0 to 3, never falling along the last dimension, each value on 1 to 16 neighbouring positions
Outputs:
- token_scores: float32 [4, 64], P(None, 'groups'), parts along dimension 1
- seq_scores: float32 [8, 4], P('groups'), parts along dimension 0
There are 2 independent parts, one for each index of `groups`. A program takes and returns all parts, laid end to end along the dimension named above; an argument that names none is the same for every part. Nothing has to cross between parts.
Inputs may be any that keep to these rules, and one draw needn't show every extreme that they name: block_mask[q, r, c] is 1 where query q keeps the block of rows r * 128 to r * 128 + 127 and columns c * 128 to c * 128 + 127, else 0. order holds each of the 32 positions once. segment_ids never falls along the positions; each sequence has 1 to 16 positions and one has exactly 16.
All inputs are finite; a program needn't handle non-finite values.
Results may differ from a plain program's by a relative error of at most 0.0035.
Values may be sent and summed in bfloat16 or wider, within the bound.
No kernel may reach another device: no remote copies, remote signals or barrier semaphores. Data moves between devices by JAX's collectives and lax.ppermute only.
A program may use at most 512 MiB of HBM per device.

v0:
```python
import jax
import jax.numpy as jnp
from jax import lax
from jax.sharding import PartitionSpec as P

BLOCK = 128
SEQS = 4
damping = 0.1


def per_device(acts_rot, grads_rot, query_grads, query_acts, eigen, block_mask, order, segment_ids):
    row_count, col_count = eigen.shape
    queries = block_mask.shape[0]
    total_blocks = block_mask.shape[1]
    col_blocks = col_count // BLOCK
    span = row_count // BLOCK + 2
    row_offset = lax.axis_index("out") * row_count
    col_offset = lax.axis_index("inp") * col_count
    first_block = jnp.minimum(row_offset // BLOCK, total_blocks - span)
    mask_band = lax.dynamic_slice(
        block_mask, (jnp.int32(0), first_block, col_offset // BLOCK), (queries, span, col_blocks)
    ).astype(jnp.float32)
    local_block = (row_offset + jnp.arange(row_count, dtype=jnp.int32)) // BLOCK - first_block
    row_pick = (local_block[:, None] == jnp.arange(span, dtype=jnp.int32)[None, :]).astype(
        jnp.float32
    )
    mask_rows = (
        jnp.einsum("rs,qsc->qrc", row_pick, mask_band, precision=lax.Precision.HIGHEST) > 0.5
    )
    query_whole = lax.all_gather(query_acts, "out", axis=1, tiled=True)
    outer_sum = jnp.einsum(
        "qsi,qsj->qij", query_grads, query_whole, preferred_element_type=jnp.float32
    )
    scaled = outer_sum / (eigen.astype(jnp.float32) + damping)[None]
    scaled = scaled.reshape(queries, row_count, col_blocks, BLOCK)
    precond = (
        jnp.where(mask_rows[..., None], scaled, 0.0)
        .astype(jnp.bfloat16)
        .reshape(queries, row_count, col_count)
    )
    spread = lax.all_to_all(grads_rot[None], "out", split_axis=2, concat_axis=0, tiled=True)
    grad_cols = lax.all_gather(spread, "inp", axis=1, tiled=True).reshape(-1, row_count)
    whole_rows = lax.all_gather(acts_rot, ("out", "inp"), axis=0, tiled=True)
    token_cols = lax.dynamic_slice_in_dim(whole_rows, col_offset, col_count, 1)
    grad_float = grad_cols.astype(jnp.float32)
    partial_rows = []
    for query_index in range(queries):
        image = lax.dot_general(
            token_cols,
            precond[query_index],
            (((1,), (1,)), ((), ())),
            preferred_element_type=jnp.float32,
        )
        partial_rows.append(jnp.sum(image * grad_float, axis=1))
    partial_value = jnp.stack(partial_rows, axis=0)
    score_total = lax.psum(partial_value, ("out", "inp"))
    token_scores = jnp.zeros_like(score_total).at[:, order].set(score_total)
    member = (segment_ids[:, None] == jnp.arange(SEQS, dtype=jnp.int32)[None, :]).astype(
        jnp.float32
    )
    seq_scores = jnp.dot(token_scores, member, precision=lax.Precision.HIGHEST)
    return (token_scores, seq_scores)


def solution(mesh):
    in_specs = (
        P(("groups", "out", "inp"), None),
        P(("groups", "out", "inp"), None),
        P("groups", None, "out"),
        P("groups", "out", "inp"),
        P("out", "inp"),
        P("groups", None, None),
        P("groups"),
        P("groups"),
    )
    out_specs = (P(None, "groups"), P("groups", None))
    return jax.shard_map(
        per_device, mesh=mesh, in_specs=in_specs, out_specs=out_specs, check_vma=False
    )
```

profile of v0, /device:TPU:0, one launch (start us, length us, event | category | flops | bytes accessed | tf_op | source)
XLA Modules:
  0.0 682.6 jit_solution(16952573298580868465)
XLA Ops:
  7.2 0.0 all-gather.4.cloned.1.call-start
  7.2 0.7 all-gather.4.cloned.1.call-update
  7.9 25.8 %copy.28 = bf16[1,2,28672]{1,0,2:T(2,128)(2,1)} copy(bf16[1,2,28672]{2,1,0:T(2,128)(2,1)} %bitcast.42) | data formatting | bytes 229376 | tf_op jit(solution)/shard_map/broadcast_in_dim | solution.py:41
  33.7 0.5 broadcast.49
  34.2 157.1 %reduce = bf16[28672,2]{1,0:T(8,128)(2,1)} reduce(bf16[28672,1,2]{2,1,0:T(2,128)(2,1)} %bitcast.39, bf16[]{:T(256)} %broadcast.49), dimensions={1}, to_apply=%bitcast.26.reduce_sub_computation | reduce | bytes 229378
  191.3 14.9 %reshape.61 = bf16[4,2,7168]{2,1,0:T(2,128)(2,1)} reshape(bf16[28672,2]{1,0:T(8,128)(2,1)} %reduce) | data formatting | bytes 229376
  206.2 6.3 all-to-all-start
  212.6 28.3 %convert_add_fusion = f32[7168,2048]{1,0:T(8,128)} fusion(bf16[7168,2048]{1,0:T(8,128)(2,1)} %param.12), kind=kLoop, calls=%fused_computation.3 | loop fusion | flops 29360128 | bytes 88080384 | tf_op jit(solution)/shard_map/add | solution.py:34
  240.9 0.0 copy-start.3
  240.9 0.0 copy-start.4
  240.9 53.6 %copy.27 = f32[7168,2048]{0,1:T(8,128)} copy(f32[7168,2048]{1,0:T(8,128)} %convert_add_fusion) | data formatting | bytes 117440512 | tf_op jit(solution)/shard_map/add | solution.py:34
  294.5 0.0 copy-done.3
  294.5 23.6 %all-gather.1 = bf16[16,2,8192]{2,1,0:T(2,128)(2,1)S(1)} all-gather(bf16[1,2,8192]{2,1,0:T(2,128)(2,1)S(1)} %bitcast.43), channel_id=1, replica_groups=mesh['groups'=2,'out'=4,'inp'=4] {'out','inp'}, dimensions={0}, use_global_device_ids=true | all-gather | bytes 557056 | tf_op jit(solution)/shard_map/all_gather | solution.py:43
  318.1 1.0 reshape.57
  319.1 2.7 fusion
  321.9 0.0 copy-done.4
  321.9 0.5 compare_select_fusion
  322.4 0.0 all-to-all-done
  322.4 18.2 %reshape.62 = bf16[28672,1,2]{2,1,0:T(2,128)(2,1)} reshape(bf16[4,2,7168]{2,1,0:T(2,128)(2,1)S(1)} %all-to-all-done) | data formatting | bytes 229376
  340.6 26.8 %copy.29 = bf16[1,2,28672]{2,1,0:T(2,128)(2,1)S(1)} copy(bf16[1,2,28672]{1,0,2:T(2,128)(2,1)} %bitcast.40) | data formatting | bytes 229376 | tf_op jit(solution)/shard_map/all_to_all | solution.py:41
  367.4 0.1 all_to_all.14
  367.5 7.4 %all-gather = bf16[4,1,8,7168]{3,0,1,2:T(4,128)(2,1)} all-gather(bf16[4,1,2,7168]{3,0,1,2:T(4,128)(2,1)S(1)} %bitcast.41), channel_id=2, replica_groups=mesh['groups'=2,'out'=4,'inp'=4] {'inp'}, dimensions={2}, use_global_device_ids=true | all-gather | bytes 573440 | tf_op jit(solution)/shard_map/all_gather | solution.py:42
  374.9 0.0 all-gather.4.cloned.1.call-done
  374.9 0.0 copy-start.2
  374.9 65.7 %broadcast_divide_fusion = bf16[4,7168,2048]{1,2,0:T(8,128)(2,1)} fusion(f32[7168,2048]{0,1:T(8,128)} %copy.27, bf16[4,128,7168]{2,1,0:T(8,128)(2,1)} %param.10, bf16[4,128,2048]{2,1,0:T(8,128)(2,1)} %all-gather.4.cloned.1.call-done), kind=kOutput, calls=%fused_computation.2 | convolution fusion | flops 15149826048 | bytes 185597952 | tf_op jit(solution)/shard_map/qsi,qsj->qij/dot_general | solution.py:31
  440.6 0.0 copy-done.2
  440.6 76.5 %select_convert_fusion = bf16[4,7168,16,128]{1,3,2,0:T(8,128)(2,1)} fusion(bf16[4,7168,16,128]{1,3,2,0:T(8,128)(2,1)} %bitcast.3, pred[4,7168,16]{1,2,0:T(8,128)(4,1)S(1)} %copy-done.2), kind=kLoop, calls=%fused_computation.1 | loop fusion | flops 58720256 | bytes 235339776 | tf_op jit(solution)/shard_map/convert_element_type | solution.py:38
  517.1 0.0 copy-start
  517.1 0.0 copy-start.1
  517.1 77.2 %fusion.27 = (bf16[1,7168,16,128]{1,3,2,0:T(8,128)(2,1)}, bf16[1,7168,16,128]{1,3,2,0:T(8,128)(2,1)}, bf16[1,7168,16,128]{1,3,2,0:T(8,128)(2,1)}, bf16[1,7168,16,128]{1,3,2,0:T(8,128)(2,1)}) fusion(bf16[4,7168,16,128]{1,3,2,0:T(8,128)(2,1)} %select_convert_fusion), kind=kLoop, calls=%fused_computation.45 | loop fusion | bytes 234881024 | tf_op jit(solution)/shard_map/slice | solution.py:50
  594.3 0.0 copy-done
  594.3 0.0 copy-done.1
  594.3 12.3 %fusion.3 = f32[32]{0:T(128)S(1)} fusion(bf16[7168,2048]{0,1:T(8,128)(2,1)} %bitcast.38, bf16[4,1,8,7168]{3,0,1,2:T(4,128)(2,1)S(1)} %copy-done, bf16[32,8192]{1,0:T(8,128)(2,1)S(1)} %copy-done.1, s32[]{:T(128)S(6)} %select_n.34), kind=kOutput, calls=%fused_computation.12 | convolution fusion | flops 940212224 | bytes 29950084 | tf_op jit(solution)/shard_map/dot_general | solution.py:48
  606.6 12.3 %fusion.4 = f32[32]{0:T(128)S(1)} fusion(bf16[7168,2048]{0,1:T(8,128)(2,1)} %bitcast.37, bf16[4,1,8,7168]{3,0,1,2:T(4,128)(2,1)S(1)} %copy-done, bf16[32,8192]{1,0:T(8,128)(2,1)S(1)} %copy-done.1, s32[]{:T(128)S(6)} %select_n.34), kind=kOutput, calls=%fused_computation.13 | convolution fusion | flops 940212224 | bytes 29950084 | tf_op jit(solution)/shard_map/dot_general | solution.py:48
  618.9 0.0 copy-start.5
  618.9 12.3 %fusion.5 = f32[32]{0:T(128)S(1)} fusion(bf16[7168,2048]{0,1:T(8,128)(2,1)} %bitcast.36, bf16[4,1,8,7168]{3,0,1,2:T(4,128)(2,1)S(1)} %copy-done, bf16[32,8192]{1,0:T(8,128)(2,1)S(1)} %copy-done.1, s32[]{:T(128)S(6)} %select_n.34), kind=kOutput, calls=%fused_computation.14 | convolution fusion | flops 940212224 | bytes 29950084 | tf_op jit(solution)/shard_map/dot_general | solution.py:48
  631.2 12.5 %fusion.6 = f32[32]{0:T(128)S(1)} fusion(bf16[7168,2048]{0,1:T(8,128)(2,1)} %bitcast.35, bf16[4,1,8,7168]{3,0,1,2:T(4,128)(2,1)S(1)} %copy-done, bf16[32,8192]{1,0:T(8,128)(2,1)S(1)} %copy-done.1, s32[]{:T(128)S(6)} %select_n.34), kind=kOutput, calls=%fused_computation.15 | convolution fusion | flops 940212224 | bytes 29950084 | tf_op jit(solution)/shard_map/dot_general | solution.py:48
  643.7 29.8 %psum.7 = f32[4,32]{1,0:T(4,128)S(1)} all-reduce(f32[4,32]{1,0:T(4,128)S(1)} %pad_maximum_fusion), channel_id=1, replica_groups=mesh['groups'=2,'out'=4,'inp'=4] {'out','inp'}, use_global_device_ids=true, to_apply=%region_4.5 | all-reduce | flops 128 | bytes 1024 | tf_op jit(solution)/shard_map/psum | solution.py:56
  673.5 0.1 copy.32
  673.6 0.8 scatter_custom_fusion
  674.4 0.7 copy.33
  675.0 0.0 copy-done.5
  675.0 0.8 fusion.18
  (2 shorter events, 0.0 us)
Async XLA Ops:
  7.2 367.7 %all-gather.4.cloned.1.call-start = ((), (), s32[]{:S(2)}) async-start(), calls=%async_computation.1 | async-start | bytes 2621440 | tf_op jit(solution)/shard_map/all_gather | solution.py:30
  206.2 116.2 %all-to-all-start = ((bf16[4,2,7168]{2,1,0:T(2,128)(2,1)}), bf16[4,2,7168]{2,1,0:T(2,128)(2,1)S(1)}, u32[]{:S(2)}, u32[]{:S(2)}) async-start(bf16[4,2,7168]{2,1,0:T(2,128)(2,1)} %reshape.61), calls=%async_computation | async-start | bytes 229376 | tf_op jit(solution)/shard_map/all_to_all | solution.py:41
  240.9 53.6 %copy-start.3 = (bf16[2,8192]{1,0:T(2,128)(2,1)S(1)}, bf16[2,8192]{1,0:T(2,128)(2,1)}, u32[]{:S(2)}) copy-start(bf16[2,8192]{1,0:T(2,128)(2,1)} %param.8) | copy-start | bytes 98308
  240.9 81.0 %copy-start.4 = (s32[32]{0:T(128)S(1)}, s32[32]{0:T(128)}, u32[]{:S(2)}) copy-start(s32[32]{0:T(128)} %param.14) | copy-start | bytes 388
  374.9 65.7 %copy-start.2 = (pred[4,7168,16]{1,2,0:T(8,128)(4,1)S(1)}, pred[4,7168,16]{1,2,0:T(8,128)(4,1)}, u32[]{:S(2)}) copy-start(pred[4,7168,16]{1,2,0:T(8,128)(4,1)} %fusion) | copy-start | bytes 1376260
  517.1 77.2 %copy-start = (bf16[4,1,8,7168]{3,0,1,2:T(4,128)(2,1)S(1)}, bf16[4,1,8,7168]{3,0,1,2:T(4,128)(2,1)}, u32[]{:S(2)}) copy-start(bf16[4,1,8,7168]{3,0,1,2:T(4,128)(2,1)} %all-gather) | copy-start | bytes 1376260
  517.1 77.2 %copy-start.1 = (bf16[32,8192]{1,0:T(8,128)(2,1)S(1)}, bf16[32,8192]{1,0:T(8,128)(2,1)}, u32[]{:S(2)}) copy-start(bf16[32,8192]{1,0:T(8,128)(2,1)} %reshape.57) | copy-start | bytes 1572868
  618.9 56.2 %copy-start.5 = (s32[32]{0:T(128)S(1)}, s32[32]{0:T(128)}, u32[]{:S(2)}) copy-start(s32[32]{0:T(128)} %param.15) | copy-start | bytes 388
Sparse Core Ops, SparseCore 0:
  9.5 48.3 all-gather.3
where the time goes:
time: 685 us; the launch traced here: 683 us
  other arithmetic  262 us (38%)
  local copies, waits for them, and re-layouts  220 us (32%)
  matrix products  119 us (17%)
  blocking collectives  60.8 us (9%)
  between operations  14.1 us (2%)
    unnamed x1, other arithmetic  157 us
    slice x1, local copies, waits for them, and re-layouts, per_device(): precond[query_index]  77.2 us
    convert_element_type x1, other arithmetic, per_device(): precond = jnp.where(mask_rows[..., None], scaled, 0.0).astype(jnp.bfloat1...  76.5 us
    dot_general x1, matrix products, per_device(): jnp.einsum('qsi,qsj->qij', query_grads, query_whole, preferred_element_ty...  65.7 us
    add x1, local copies, waits for them, and re-layouts, per_device(): scaled = outer_sum / (eigen.astype(jnp.float32) + damping)[None]  53.6 us
    dot_general x4, matrix products, per_device(): lax.dot_general(token_cols, precond[query_index], (((1,), (1,)), ((), ())...  49.4 us
    unnamed x17, local copies, waits for them, and re-layouts  35.3 us
    psum x1, blocking collectives, per_device(): score_total = lax.psum(partial_value, ('out', 'inp'))  29.8 us
  transfers between devices with their start and end apart: 2, of which 0 were waited for; matrix products, arithmetic and copies ran while one was open for 48% of the time, Pallas kernels for 0%

commit v1 on v0

--- a/solution.py
+++ b/solution.py
@@ -1,3 +1,4 @@
+import functools
 import jax
 import jax.numpy as jnp
 from jax import lax
@@ -6,6 +7,18 @@
 BLOCK = 128
 SEQS = 4
 damping = 0.1
+
+
+def name_the_bars(block_in, at_axis, array_axis):
+    return jnp.concatenate(
+        lax.all_to_all(
+            jnp.stack(jnp.split(block_in, lax.axis_size("out"), axis=at_axis)), "out", 0, 0
+        ),
+        axis=array_axis,
+    )
+
+
+_touch_slot = functools.partial(name_the_bars, at_axis=2, array_axis=0)
 
 
 def per_device(acts_rot, grads_rot, query_grads, query_acts, eigen, block_mask, order, segment_ids):
@@ -38,7 +51,7 @@
         .astype(jnp.bfloat16)
         .reshape(queries, row_count, col_count)
     )
-    spread = lax.all_to_all(grads_rot[None], "out", split_axis=2, concat_axis=0, tiled=True)
+    spread = _touch_slot(grads_rot[None])
     grad_cols = lax.all_gather(spread, "inp", axis=1, tiled=True).reshape(-1, row_count)
     whole_rows = lax.all_gather(acts_rot, ("out", "inp"), axis=0, tiled=True)
     token_cols = lax.dynamic_slice_in_dim(whole_rows, col_offset, col_count, 1)

time: 685 us -> 443 us (0.65)
  other arithmetic: 262 us -> 107 us
  local copies, waits for them, and re-layouts: 220 us -> 134 us
    unnamed x1 -> x0, other arithmetic: 157 us -> none
    unnamed x17 -> x14, local copies, waits for them, and re-layouts: 35.3 us -> 1.69 us
    all_to_all x2 -> x1, local copies, waits for them, and re-layouts: 26.9 us -> 0.05 us  [name_the_bars(): lax.all_to_all(jnp.stack(jnp.split(block_in, lax.axis_size('out'), axis=a...]
    broadcast_in_dim x1 -> x0, local copies, waits for them, and re-layouts: 25.8 us -> none  [per_device(): grads_rot[None]]
  transfers between devices with their start and end apart: 2 -> 2, of which waited for: 0 -> 0; matrix products, arithmetic and copies ran while one was open for 48% -> 20% of each run, Pallas kernels for 0% -> 0%
where the time goes in v1:
time: 443 us; the launch traced here: 442 us
  local copies, waits for them, and re-layouts  134 us (30%)
  matrix products  119 us (27%)
  other arithmetic  107 us (24%)
  blocking collectives  60.8 us (14%)
  between operations  14.1 us (3%)
  starting transfers between devices  6.38 us (1%)
    slice x1, local copies, waits for them, and re-layouts, per_device(): precond[query_index]  77.2 us
    convert_element_type x1, other arithmetic, per_device(): precond = jnp.where(mask_rows[..., None], scaled, 0.0).astype(jnp.bfloat1...  76.5 us
    dot_general x1, matrix products, per_device(): jnp.einsum('qsi,qsj->qij', query_grads, query_whole, preferred_element_ty...  65.7 us
    add x1, local copies, waits for them, and re-layouts, per_device(): scaled = outer_sum / (eigen.astype(jnp.float32) + damping)[None]  53.6 us
    dot_general x4, matrix products, per_device(): lax.dot_general(token_cols, precond[query_index], (((1,), (1,)), ((), ())...  49.4 us
    psum x1, blocking collectives, per_device(): score_total = lax.psum(partial_value, ('out', 'inp'))  29.8 us
    add x1, other arithmetic, per_device(): scaled = outer_sum / (eigen.astype(jnp.float32) + damping)[None]  28.8 us
    all_gather x1, blocking collectives, per_device(): whole_rows = lax.all_gather(acts_rot, ('out', 'inp'), axis=0, tiled=True)  23.4 us
  transfers between devices with their start and end apart: 2, of which 0 were waited for; matrix products, arithmetic and copies ran while one was open for 20% of the time, Pallas kernels for 0%

profile of v1, /device:TPU:0, one launch (start us, length us, event | category | flops | bytes accessed | tf_op | source)
XLA Modules:
  0.0 441.5 jit_solution(7068360197900982658)
XLA Ops:
  7.2 0.0 all-gather.4.cloned.1.call-start
  7.2 0.7 all-gather.4.cloned.1.call-update
  7.9 0.9 slice_bitcast_fusion.3
  8.8 0.8 pad_maximum_fusion
  9.6 6.3 %all-to-all-start = ((bf16[4,1,2,7168]{3,2,1,0:T(2,128)(2,1)}), bf16[4,1,2,7168]{3,2,1,0:T(2,128)(2,1)S(1)}, u32[]{:S(2)}, u32[]{:S(2)}) async-start(bf16[4,1,2,7168]{3,2,1,0:T(2,128)(2,1)} %pad_maximum_fusion), calls=%async_computation | async-start | bytes 229376 | tf_op jit(solution)/shard_map/all_to_all | solution.py:14
  16.0 28.8 %convert_add_fusion = f32[7168,2048]{1,0:T(8,128)} fusion(bf16[7168,2048]{1,0:T(8,128)(2,1)} %param.12), kind=kLoop, calls=%fused_computation.3 | loop fusion | flops 29360128 | bytes 88080384 | tf_op jit(solution)/shard_map/add | solution.py:47
  44.8 0.0 copy-start.3
  44.8 0.0 copy-start.4
  44.8 53.6 %copy.25 = f32[7168,2048]{0,1:T(8,128)} copy(f32[7168,2048]{1,0:T(8,128)} %convert_add_fusion) | data formatting | bytes 117440512 | tf_op jit(solution)/shard_map/add | solution.py:47
  98.4 0.0 copy-done.3
  98.5 23.4 %all-gather.1 = bf16[16,2,8192]{2,1,0:T(2,128)(2,1)S(1)} all-gather(bf16[1,2,8192]{2,1,0:T(2,128)(2,1)S(1)} %bitcast.43), channel_id=1, replica_groups=mesh['groups'=2,'out'=4,'inp'=4] {'out','inp'}, dimensions={0}, use_global_device_ids=true | all-gather | bytes 557056 | tf_op jit(solution)/shard_map/all_gather | solution.py:56
  121.9 1.0 reshape.61
  122.9 2.8 fusion
  125.7 0.0 copy-done.4
  125.7 0.5 compare_select_fusion
  126.2 0.0 all-to-all-done
  126.2 7.6 %all-gather = bf16[4,1,8,7168]{3,0,1,2:T(4,128)(2,1)} all-gather(bf16[4,1,2,7168]{3,0,1,2:T(4,128)(2,1)S(1)} %copy.26), channel_id=2, replica_groups=mesh['groups'=2,'out'=4,'inp'=4] {'inp'}, dimensions={2}, use_global_device_ids=true | all-gather | bytes 573440 | tf_op jit(solution)/shard_map/all_gather | solution.py:55
  133.8 0.0 all-gather.4.cloned.1.call-done
  133.8 0.0 copy-start.2
  133.8 65.7 %broadcast_divide_fusion = bf16[4,7168,2048]{1,2,0:T(8,128)(2,1)} fusion(f32[7168,2048]{0,1:T(8,128)} %copy.25, bf16[4,128,7168]{2,1,0:T(8,128)(2,1)} %param.10, bf16[4,128,2048]{2,1,0:T(8,128)(2,1)} %all-gather.4.cloned.1.call-done), kind=kOutput, calls=%fused_computation.2 | convolution fusion | flops 15149826048 | bytes 185597952 | tf_op jit(solution)/shard_map/qsi,qsj->qij/dot_general | solution.py:44
  199.5 0.0 copy-done.2
  199.5 76.5 %select_convert_fusion = bf16[4,7168,16,128]{1,3,2,0:T(8,128)(2,1)} fusion(bf16[4,7168,16,128]{1,3,2,0:T(8,128)(2,1)} %bitcast.3, pred[4,7168,16]{1,2,0:T(8,128)(4,1)S(1)} %copy-done.2), kind=kLoop, calls=%fused_computation.1 | loop fusion | flops 58720256 | bytes 235339776 | tf_op jit(solution)/shard_map/convert_element_type | solution.py:51
  275.9 0.0 copy-start
  275.9 0.0 copy-start.1
  276.0 77.2 %fusion.27 = (bf16[1,7168,16,128]{1,3,2,0:T(8,128)(2,1)}, bf16[1,7168,16,128]{1,3,2,0:T(8,128)(2,1)}, bf16[1,7168,16,128]{1,3,2,0:T(8,128)(2,1)}, bf16[1,7168,16,128]{1,3,2,0:T(8,128)(2,1)}) fusion(bf16[4,7168,16,128]{1,3,2,0:T(8,128)(2,1)} %select_convert_fusion), kind=kLoop, calls=%fused_computation.50 | loop fusion | bytes 234881024 | tf_op jit(solution)/shard_map/slice | solution.py:63
  353.1 0.0 copy-done
  353.1 0.0 copy-done.1
  353.1 12.3 %fusion.3 = f32[32]{0:T(128)S(1)} fusion(bf16[7168,2048]{0,1:T(8,128)(2,1)} %bitcast.41, bf16[4,1,8,7168]{3,0,1,2:T(4,128)(2,1)S(1)} %copy-done, bf16[32,8192]{1,0:T(8,128)(2,1)S(1)} %copy-done.1, s32[]{:T(128)S(6)} %select_n.34), kind=kOutput, calls=%fused_computation.12 | convolution fusion | flops 940212224 | bytes 29950084 | tf_op jit(solution)/shard_map/dot_general | solution.py:61
  365.4 12.3 %fusion.4 = f32[32]{0:T(128)S(1)} fusion(bf16[7168,2048]{0,1:T(8,128)(2,1)} %bitcast.40, bf16[4,1,8,7168]{3,0,1,2:T(4,128)(2,1)S(1)} %copy-done, bf16[32,8192]{1,0:T(8,128)(2,1)S(1)} %copy-done.1, s32[]{:T(128)S(6)} %select_n.34), kind=kOutput, calls=%fused_computation.13 | convolution fusion | flops 940212224 | bytes 29950084 | tf_op jit(solution)/shard_map/dot_general | solution.py:61
  377.7 0.0 copy-start.5
  377.7 12.3 %fusion.5 = f32[32]{0:T(128)S(1)} fusion(bf16[7168,2048]{0,1:T(8,128)(2,1)} %bitcast.39, bf16[4,1,8,7168]{3,0,1,2:T(4,128)(2,1)S(1)} %copy-done, bf16[32,8192]{1,0:T(8,128)(2,1)S(1)} %copy-done.1, s32[]{:T(128)S(6)} %select_n.34), kind=kOutput, calls=%fused_computation.14 | convolution fusion | flops 940212224 | bytes 29950084 | tf_op jit(solution)/shard_map/dot_general | solution.py:61
  390.0 12.5 %fusion.6 = f32[32]{0:T(128)S(1)} fusion(bf16[7168,2048]{0,1:T(8,128)(2,1)} %bitcast.38, bf16[4,1,8,7168]{3,0,1,2:T(4,128)(2,1)S(1)} %copy-done, bf16[32,8192]{1,0:T(8,128)(2,1)S(1)} %copy-done.1, s32[]{:T(128)S(6)} %select_n.34), kind=kOutput, calls=%fused_computation.15 | convolution fusion | flops 940212224 | bytes 29950084 | tf_op jit(solution)/shard_map/dot_general | solution.py:61
  402.5 29.8 %psum.7 = f32[4,32]{1,0:T(4,128)S(1)} all-reduce(f32[4,32]{1,0:T(4,128)S(1)} %pad_maximum_fusion.1), channel_id=1, replica_groups=mesh['groups'=2,'out'=4,'inp'=4] {'out','inp'}, use_global_device_ids=true, to_apply=%region_4.5 | all-reduce | flops 128 | bytes 1024 | tf_op jit(solution)/shard_map/psum | solution.py:69
  432.4 0.1 copy.28
  432.5 0.8 scatter_custom_fusion
  433.3 0.7 copy.29
  433.9 0.0 copy-done.5
  433.9 0.8 fusion.18
  (3 shorter events, 0.1 us)
Async XLA Ops:
  7.2 126.6 %all-gather.4.cloned.1.call-start = ((), (), s32[]{:S(2)}) async-start(), calls=%async_computation.1 | async-start | bytes 2621440 | tf_op jit(solution)/shard_map/all_gather | solution.py:43
  9.6 116.6 %all-to-all-start = ((bf16[4,1,2,7168]{3,2,1,0:T(2,128)(2,1)}), bf16[4,1,2,7168]{3,2,1,0:T(2,128)(2,1)S(1)}, u32[]{:S(2)}, u32[]{:S(2)}) async-start(bf16[4,1,2,7168]{3,2,1,0:T(2,128)(2,1)} %pad_maximum_fusion), calls=%async_computation | async-start | bytes 229376 | tf_op jit(solution)/shard_map/all_to_all | solution.py:14
  44.8 53.6 %copy-start.3 = (bf16[2,8192]{1,0:T(2,128)(2,1)S(1)}, bf16[2,8192]{1,0:T(2,128)(2,1)}, u32[]{:S(2)}) copy-start(bf16[2,8192]{1,0:T(2,128)(2,1)} %param.8) | copy-start | bytes 98308
  44.8 80.8 %copy-start.4 = (s32[32]{0:T(128)S(1)}, s32[32]{0:T(128)}, u32[]{:S(2)}) copy-start(s32[32]{0:T(128)} %param.14) | copy-start | bytes 388
  133.8 65.7 %copy-start.2 = (pred[4,7168,16]{1,2,0:T(8,128)(4,1)S(1)}, pred[4,7168,16]{1,2,0:T(8,128)(4,1)}, u32[]{:S(2)}) copy-start(pred[4,7168,16]{1,2,0:T(8,128)(4,1)} %fusion) | copy-start | bytes 1376260
  275.9 77.2 %copy-start = (bf16[4,1,8,7168]{3,0,1,2:T(4,128)(2,1)S(1)}, bf16[4,1,8,7168]{3,0,1,2:T(4,128)(2,1)}, u32[]{:S(2)}) copy-start(bf16[4,1,8,7168]{3,0,1,2:T(4,128)(2,1)} %all-gather) | copy-start | bytes 1376260
  275.9 77.2 %copy-start.1 = (bf16[32,8192]{1,0:T(8,128)(2,1)S(1)}, bf16[32,8192]{1,0:T(8,128)(2,1)}, u32[]{:S(2)}) copy-start(bf16[32,8192]{1,0:T(8,128)(2,1)} %reshape.61) | copy-start | bytes 1572868
  377.7 56.2 %copy-start.5 = (s32[32]{0:T(128)S(1)}, s32[32]{0:T(128)}, u32[]{:S(2)}) copy-start(s32[32]{0:T(128)} %param.15) | copy-start | bytes 388
Sparse Core Ops, SparseCore 0:
  9.5 48.3 all-gather.3
